TPU v7x, 32 devices: a whole 2x2x4 slice. The times are simulated.
32 devices in a mesh: grp: 2 (over x), chan: 16 (over z, y, core).
Axes of the slice: x: 2, y: 2, z: 4, core: 2. Of those that a mesh axis runs over, the one named last changes fastest.
Arguments:
- samples: bfloat16 [32, 16, 256, 1024], P(('grp', 'chan')), parts along dimension 0, may hold values from -6 to 6
- fir: float32 [16, 1024], replicated, may hold values from -1.5 to 1.5
- chan_assign: int32 [256], replicated, may hold values from 0 to 511, as said below
- input_order: int32 [1024], replicated, may hold values from 0 to 1023, each once
Outputs:
- vis: bfloat16 [512, 1024, 1024], P(('grp', 'chan')), parts along dimension 0
There are 2 independent parts, one for each index of `grp`. A program takes and returns all parts, laid end to end along the dimension named above; an argument that names none is the same for every part. Nothing has to cross between parts.
Inputs may be any that keep to these rules, and one draw needn't show every extreme that they name: `chan_assign`: distinct transform bins; bin 0 and bin 1024 // 2 - 1 are always among them. `input_order`: each input number once.
All inputs are finite; a program needn't handle non-finite values.
Results may differ from a plain program's by a relative error of at most 0.0074.
Values may be sent and summed in bfloat16 or wider, within the bound.
No kernel may reach another device: no remote copies, remote signals or barrier semaphores. Data moves between devices by JAX's collectives and lax.ppermute only.
A program may use at most 256 MiB of HBM per device.

v0:
```python
import math
import jax
import jax.numpy as jnp
from jax import lax
from jax.sharding import PartitionSpec as P

QUART = 4


def shifted(value, axis, steps):
    count = lax.axis_size(axis)
    initial, last = (max(0, -steps), min(count, count - steps))
    return lax.ppermute(value, axis, [(source, source + steps) for source in range(initial, last)])


def make_table(chan_assign, frame_len):
    samples_index = jnp.arange(frame_len, dtype=jnp.int32)
    phase_index = chan_assign[:, None] * samples_index[None, :] % frame_len
    angles = phase_index.astype(jnp.float32) * (2.0 * math.pi / frame_len)
    norm_scale = 1.0 / math.sqrt(frame_len)
    return jnp.stack([jnp.cos(angles) * norm_scale, -jnp.sin(angles) * norm_scale]).astype(
        jnp.bfloat16
    )


def on_device(samples, fir, chan_assign, input_order):
    own_frames = samples[0]
    frames_quarter, slots_dev, frame_len = own_frames.shape
    taps_count = fir.shape[0]
    chan_count = lax.axis_size("chan")
    group_count = chan_count // QUART
    history_len = taps_count - 1
    lead_len = min(frames_quarter, history_len)
    tail_frames = own_frames[frames_quarter - lead_len :]
    pieces = shifted(tail_frames, "chan", 1 * group_count)
    extended = jnp.concatenate([pieces, own_frames], axis=0)
    dft_table = make_table(chan_assign, frame_len)
    chan_total = chan_assign.shape[0]
    chan_dev = chan_total // chan_count
    inputs_all = input_order.shape[0]
    inverse = jnp.argsort(input_order)
    spectra_total = QUART * frames_quarter
    accum = jnp.zeros((frames_quarter, slots_dev, frame_len), jnp.float32)
    for tap_index in range(taps_count):
        begin = 0 + history_len - tap_index
        accum = accum + fir[tap_index][None, None, :] * extended[
            begin : begin + frames_quarter
        ].astype(jnp.float32)
    filtered = accum.astype(jnp.bfloat16)
    spectra = jnp.einsum("pcn,fin->cfpi", dft_table, filtered, preferred_element_type=jnp.float32)
    spectra = spectra.astype(jnp.bfloat16).reshape(
        chan_count, chan_dev, frames_quarter, 2, slots_dev
    )
    received = lax.all_to_all(spectra, "chan", split_axis=0, concat_axis=4, tiled=True)
    items = received.shape[1]
    row_count = received.shape[2]
    split_parts = received.reshape(items, row_count, 2, QUART, inputs_all)
    ordered = jnp.take(split_parts, inverse, axis=4)
    stacked = ordered.reshape(items, row_count * 2 * QUART, inputs_all)
    real_rows = ordered[:, :, 0].reshape(items, row_count * QUART, inputs_all)
    imag_rows = ordered[:, :, 1].reshape(items, row_count * QUART, inputs_all)
    auto_sum = jnp.einsum("kra,krb->kab", stacked, stacked, preferred_element_type=jnp.float32)
    cross_sum = jnp.einsum("kra,krb->kab", real_rows, imag_rows, preferred_element_type=jnp.float32)
    row_index = lax.broadcasted_iota(jnp.int32, (inputs_all, inputs_all), 0)
    col_index = lax.broadcasted_iota(jnp.int32, (inputs_all, inputs_all), 1)
    upper_mask = (row_index <= col_index)[None, :, :]
    packed = (
        jnp.where(upper_mask, auto_sum, cross_sum - jnp.swapaxes(cross_sum, 1, 2)) / spectra_total
    )
    return packed.astype(jnp.bfloat16)


def solution(mesh):
    in_specs = (P(("grp", "chan"), None, None, None), P(), P(), P())
    out_specs = P(("grp", "chan"), None, None)
    return jax.shard_map(
        on_device, mesh=mesh, in_specs=in_specs, out_specs=out_specs, check_vma=False
    )
```

profile of v0, /device:TPU:13, one launch (start us, length us, event | category | flops | bytes accessed | tf_op | source)
XLA Modules:
  0.0 708.8 jit_solution(15074221744417982181)
XLA Ops:
  0.0 4.2 slice_bitcast_fusion
  4.2 3.2 collective-permute-start
  7.4 1.3 fusion.34
  8.7 5.6 multiply_convert_fusion.1
  14.3 161.9 %collective-permute-done = bf16[15,256,1024]{2,1,0:T(8,128)(2,1)} collective-permute-done((bf16[15,256,1024]{2,1,0:T(8,128)(2,1)S(1)}, bf16[15,256,1024]{2,1,0:T(8,128)(2,1)}, u32[]{:S(2)}, u32[]{:S(2)}) %collective-permute-start) | collective-permute-done | bytes 7864352 | tf_op jit(solution)/shard_map/ppermute | solution.py:13
  176.3 58.6 %fusion.41 = bf16[16,256,1024,1]{2,1,3,0:T(8,128)(2,1)} fusion(bf16[16,256,1024]{2,1,0:T(8,128)(2,1)} %bitcast.64, bf16[15,256,1024]{2,1,0:T(8,128)(2,1)} %collective-permute-done, f32[1024]{0:T(1024)S(1)} %bitcast.80, f32[1024]{0:T(1024)S(1)} %bitcast.81, f32[1024]{0:T(1024)S(1)} %bitcast.67, f32[1024]{0:T(1024)S(1)} %bitcast.68, ...), kind=kLoop, calls=%fused_computation.51.clone.clone.clone.2 | loop fusion | flops 264241152 | bytes 24707072 | tf_op jit(solution)/shard_map/pcn,fin->cfpi/dot_general | solution.py:50
  234.9 8.2 %fusion.20 = bf16[16,256,2,256]{1,3,2,0:T(8,128)(2,1)S(1)} fusion(bf16[1,256,1024]{2,1,0:T(8,128)(2,1)S(1)} %get-tuple-element.26, bf16[1,256,1024]{2,1,0:T(8,128)(2,1)S(1)} %get-tuple-element.25, bf16[16,256,1024,1]{2,1,3,0:T(8,128)(2,1)} %fusion.41), kind=kOutput, calls=%fused_computation.56 | convolution fusion | flops 4299161600 | bytes 13631488 | tf_op jit(solution)/shard_map/pcn,fin->cfpi/dot_general | solution.py:50
  243.1 0.0 copy-start
  243.1 6.5 copy.16
  249.6 7.4 %all-to-all-start = ((bf16[16,16,16,2,256]{4,3,2,1,0:T(2,128)(2,1)}), bf16[16,16,16,2,256]{4,3,2,1,0:T(2,128)(2,1)}, u32[]{:S(2)}, u32[]{:S(2)}) async-start(bf16[16,16,16,2,256]{4,3,2,1,0:T(2,128)(2,1)} %copy.16), calls=%async_computation | async-start | bytes 8388608 | tf_op jit(solution)/shard_map/all_to_all | solution.py:54
  257.0 0.0 copy-done
  257.0 4.4 sort.17
  261.3 0.3 iota_compare_fusion
  261.7 87.7 %all-to-all-done = bf16[16,16,16,2,256]{4,3,2,1,0:T(2,128)(2,1)} async-done(((bf16[16,16,16,2,256]{4,3,2,1,0:T(2,128)(2,1)}), bf16[16,16,16,2,256]{4,3,2,1,0:T(2,128)(2,1)}, u32[]{:S(2)}, u32[]{:S(2)}) %all-to-all-start) | async-done | bytes 4194336 | tf_op jit(solution)/shard_map/all_to_all | solution.py:54
  349.4 32.4 %copy.26 = bf16[1,16,16,2,16,256]{2,1,5,4,3,0:T(8,128)(2,1)} copy(bf16[1,16,16,2,16,256]{5,3,2,1,4,0:T(2,128)(2,1)} %bitcast.24) | data formatting | bytes 8388608 | tf_op jit(solution)/shard_map/reshape | solution.py:57
  381.8 36.7 %gather_fusion = bf16[1024,16,16,2,4]{2,1,4,3,0:T(8,128)(2,1)} fusion(bf16[16,16,2,4,1024]{1,0,4,3,2:T(8,128)(2,1)} %bitcast.63, s32[1024]{0:T(1024)S(1)} %fusion.31), kind=kCustom, calls=%fused_computation | custom fusion | bytes 8392704 | tf_op jit(solution)/shard_map/jit(_take)/gather | solution.py:58
  418.4 35.7 %copy.19 = bf16[16,16,2,4,1024]{4,0,3,2,1:T(8,128)(2,1)} copy(bf16[16,16,2,4,1024]{1,0,3,2,4:T(8,128)(2,1)} %bitcast.62) | data formatting | bytes 8388608 | tf_op jit(solution)/shard_map/jit(_take)/gather | solution.py:58
  454.1 22.7 %broadcast_select_fusion = bf16[16,16,2,4,1024]{1,0,3,2,4:T(8,128)(2,1)} fusion(pred[1024]{0:T(1024)(128)(4,1)S(1)} %compare_and_fusion, bf16[1024,16,16,2,4]{2,1,4,3,0:T(8,128)(2,1)} %gather_fusion), kind=kLoop, calls=%fused_computation.33 | loop fusion | flops 2097152 | bytes 8389632 | tf_op jit(solution)/shard_map/jit(_take)/select_n | solution.py:58
  476.9 4.5 bitcast_select_fusion
  481.3 25.2 %fusion.33 = (bf16[16,16,1,4,1024]{1,0,3,2,4:T(8,128)(2,1)}, bf16[16,16,1,4,1024]{1,0,3,2,4:T(8,128)(2,1)}) fusion(bf16[16,16,2,4,1024]{1,0,3,2,4:T(8,128)(2,1)} %broadcast_select_fusion), kind=kLoop, calls=%fused_computation.75 | loop fusion | bytes 8388608 | tf_op jit(solution)/shard_map/slice | solution.py:61
  506.6 21.9 %copy.23 = bf16[16,16,1,4,1024]{4,3,1,0,2:T(4,128)(2,1)} copy(bf16[16,16,1,4,1024]{1,0,3,2,4:T(8,128)(2,1)} %get-tuple-element.7) | data formatting | bytes 4194304 | tf_op jit(solution)/shard_map/slice | solution.py:61
  528.5 2.5 reshape_squeeze.7
  531.0 21.9 %copy.22 = bf16[16,16,1,4,1024]{4,3,1,0,2:T(4,128)(2,1)} copy(bf16[16,16,1,4,1024]{1,0,3,2,4:T(8,128)(2,1)} %get-tuple-element.8) | data formatting | bytes 4194304 | tf_op jit(solution)/shard_map/slice | solution.py:60
  552.9 4.0 reshape_squeeze.6
  556.9 24.8 %fusion.35 = f32[16,1024,1024]{2,1,0:T(8,128)} fusion(bf16[16,64,1024]{2,1,0:T(8,128)(2,1)} %reshape_squeeze.6, bf16[16,64,1024]{2,1,0:T(8,128)(2,1)S(1)} %reshape_squeeze.7), kind=kOutput, calls=%fused_computation.77 | convolution fusion | flops 2147483648 | bytes 71303168 | tf_op jit(solution)/shard_map/kra,krb->kab/dot_general | solution.py:63
  581.7 62.8 %copy.24 = f32[16,1024,1024]{1,2,0:T(8,128)} copy(f32[16,1024,1024]{2,1,0:T(8,128)} %fusion.35) | data formatting | bytes 134217728 | tf_op jit(solution)/shard_map/kra,krb->kab/dot_general | solution.py:63
  644.5 64.2 %fusion.2 = bf16[16,1024,1024]{2,1,0:T(8,128)(2,1)} fusion(f32[16,1024,1024]{2,1,0:T(8,128)} %fusion.35, f32[16,1024,1024]{1,2,0:T(8,128)} %copy.24, pred[1024,1024]{1,0:T(8,128)(4,1)S(1)} %iota_compare_fusion, bf16[16,128,1024]{2,0,1:T(8,128)(2,1)} %bitcast_select_fusion), kind=kOutput, calls=%fused_computation.4 | convolution fusion | flops 4362076160 | bytes 173015040 | tf_op jit(solution)/shard_map/kra,krb->kab/dot_general | solution.py:62
  (3 shorter events, 0.0 us)
Async XLA Ops:
  4.2 172.1 %collective-permute-start = (bf16[15,256,1024]{2,1,0:T(8,128)(2,1)S(1)}, bf16[15,256,1024]{2,1,0:T(8,128)(2,1)}, u32[]{:S(2)}, u32[]{:S(2)}) collective-permute-start(bf16[15,256,1024]{2,1,0:T(8,128)(2,1)S(1)} %slice_bitcast_fusion), channel_id=1, source_target_pairs={{0,4},{1,5},{2,6},{3,7},{4,8},{5,9},{6,10},{7,11},{8,12},{9,13},{1... | collective-permute-start | bytes 23592968 | tf_op jit(solution)/shard_map/ppermute | solution.py:13
  243.1 13.9 %copy-start = (s32[1024]{0:T(1024)S(1)}, s32[1024]{0:T(1024)}, u32[]{:S(2)}) copy-start(s32[1024]{0:T(1024)} %param.7) | copy-start | bytes 12292
  249.6 99.8 %all-to-all-start = ((bf16[16,16,16,2,256]{4,3,2,1,0:T(2,128)(2,1)}), bf16[16,16,16,2,256]{4,3,2,1,0:T(2,128)(2,1)}, u32[]{:S(2)}, u32[]{:S(2)}) async-start(bf16[16,16,16,2,256]{4,3,2,1,0:T(2,128)(2,1)} %copy.16), calls=%async_computation | async-start | bytes 8388608 | tf_op jit(solution)/shard_map/all_to_all | solution.py:54
where the time goes:
time: 714 us; the launch traced here: 709 us
  local copies, waits for them, and re-layouts  255 us (36%)
  waiting for transfers between devices  250 us (35%)
  matrix products  97.2 us (14%)
  other arithmetic  96.2 us (13%)
  starting transfers between devices  10.6 us (1%)
    ppermute x1, waiting for transfers between devices, shifted(): lax.ppermute(value, axis, [(source, source + steps) for source in range(i...  162 us
    all_to_all x1, waiting for transfers between devices, on_device(): lax.all_to_all(spectra, 'chan', split_axis=0, concat_axis=4, tiled=True)  87.7 us
    gather x2, local copies, waits for them, and re-layouts, on_device(): ordered = jnp.take(split_parts, inverse, axis=4)  72.4 us
    dot_general x1, matrix products, on_device(): jnp.einsum('kra,krb->kab', stacked, stacked, preferred_element_type=jnp.f...  64.2 us
    dot_general x1, local copies, waits for them, and re-layouts, on_device(): jnp.einsum('kra,krb->kab', real_rows, imag_rows, preferred_element_type=j...  62.8 us
    dot_general x1, other arithmetic, on_device(): jnp.einsum('pcn,fin->cfpi', dft_table, filtered, preferred_element_type=j...  58.6 us
    slice x2, local copies, waits for them, and re-layouts, on_device(): imag_rows = ordered[:, :, 1].reshape(items, row_count * QUART, inputs_all)  47.1 us
    reshape x1, local copies, waits for them, and re-layouts, on_device(): split_parts = received.reshape(items, row_count, 2, QUART, inputs_all)  32.4 us
  transfers between devices with their start and end apart: 2, of which 2 were waited for; matrix products, arithmetic and copies ran while one was open for 2% of the time, Pallas kernels for 0%

commit v1 on v0

--- a/solution.py
+++ b/solution.py
@@ -5,6 +5,22 @@
 from jax.sharding import PartitionSpec as P
 
 QUART = 4
+
+
+def exchange_in_pairs(value, axis, split, join):
+    ways, here = (lax.axis_size(axis), lax.axis_index(axis))
+    width = value.shape[split] // ways
+    shape = list(value.shape)
+    shape[split] = width
+    height = shape[join]
+    shape[join] = height * ways
+    full = jnp.zeros(shape, value.dtype)
+    for mask in range(ways):
+        part = lax.dynamic_slice_in_dim(value, (here ^ mask) * width, width, axis=split)
+        if mask:
+            part = lax.ppermute(part, axis, [(d, d ^ mask) for d in range(ways)])
+        full = lax.dynamic_update_slice_in_dim(full, part, (here ^ mask) * height, axis=join)
+    return full
 
 
 def shifted(value, axis, steps):
@@ -51,7 +67,7 @@
     spectra = spectra.astype(jnp.bfloat16).reshape(
         chan_count, chan_dev, frames_quarter, 2, slots_dev
     )
-    received = lax.all_to_all(spectra, "chan", split_axis=0, concat_axis=4, tiled=True)
+    received = exchange_in_pairs(spectra, "chan", 0, 4)
     items = received.shape[1]
     row_count = received.shape[2]
     split_parts = received.reshape(items, row_count, 2, QUART, inputs_all)

time: 714 us -> 780 us (1.092)
  the two profiles are of different devices: /device:TPU:13 before, /device:TPU:0 now
where the time goes in v1:
time: 780 us; the launch traced here: 767 us
  local copies, waits for them, and re-layouts  342 us (44%)
  waiting for transfers between devices  199 us (26%)
  other arithmetic  97.4 us (12%)
  matrix products  97.2 us (12%)
  starting transfers between devices  30.5 us (4%)
    ppermute x1, waiting for transfers between devices, shifted(): lax.ppermute(value, axis, [(source, source + steps) for source in range(i...  154 us
    gather x2, local copies, waits for them, and re-layouts, on_device(): ordered = jnp.take(split_parts, inverse, axis=4)  72.4 us
    dot_general x1, matrix products, on_device(): jnp.einsum('kra,krb->kab', stacked, stacked, preferred_element_type=jnp.f...  64.2 us
    ppermute x15, local copies, waits for them, and re-layouts, exchange_in_pairs(): part = lax.ppermute(part, axis, [(d, d ^ mask) for d in range(ways)])  63.6 us
    dot_general x1, local copies, waits for them, and re-layouts, on_device(): jnp.einsum('kra,krb->kab', real_rows, imag_rows, preferred_element_type=j...  62.9 us
    dot_general x1, other arithmetic, on_device(): jnp.einsum('pcn,fin->cfpi', dft_table, filtered, preferred_element_type=j...  58.2 us
    slice x2, local copies, waits for them, and re-layouts, on_device(): imag_rows = ordered[:, :, 1].reshape(items, row_count * QUART, inputs_all)  47.1 us
    ppermute x15, waiting for transfers between devices, exchange_in_pairs(): part = lax.ppermute(part, axis, [(d, d ^ mask) for d in range(ways)])  45.6 us
  transfers between devices with their start and end apart: 16, of which 6 were waited for; matrix products, arithmetic and copies ran while one was open for 17% of the time, Pallas kernels for 0%

profile of v1, /device:TPU:0, one launch (start us, length us, event | category | flops | bytes accessed | tf_op | source)
XLA Modules:
  0.0 766.6 jit_solution(13134633790247263691)
XLA Ops:
  0.0 7.7 %slice_bitcast_fusion = bf16[15,256,1024]{2,1,0:T(8,128)(2,1)} fusion(bf16[1,16,256,1024]{3,2,1,0:T(8,128)(2,1)} %param.4), kind=kLoop, calls=%fused_computation.52 | loop fusion | bytes 15728640 | tf_op jit(solution)/shard_map/slice | solution.py:50
  7.7 8.0 %collective-permute-start = (bf16[15,256,1024]{2,1,0:T(8,128)(2,1)}, bf16[15,256,1024]{2,1,0:T(8,128)(2,1)}, u32[]{:S(2)}, u32[]{:S(2)}) collective-permute-start(bf16[15,256,1024]{2,1,0:T(8,128)(2,1)} %slice_bitcast_fusion), channel_id=1, source_target_pairs={{0,4},{1,5},{2,6},{3,7},{4,8},{5,9},{6,10},{7,11},{8,12},{9,13},{1... | collective-permute-start | bytes 23592968 | tf_op jit(solution)/shard_map/ppermute | solution.py:29
  15.7 5.0 sort.17
  22.1 5.6 multiply_convert_fusion.1
  27.7 153.7 %collective-permute-done = bf16[15,256,1024]{2,1,0:T(8,128)(2,1)} collective-permute-done((bf16[15,256,1024]{2,1,0:T(8,128)(2,1)}, bf16[15,256,1024]{2,1,0:T(8,128)(2,1)}, u32[]{:S(2)}, u32[]{:S(2)}) %collective-permute-start) | collective-permute-done | bytes 7864352 | tf_op jit(solution)/shard_map/ppermute | solution.py:29
  181.5 58.2 %fusion.41 = bf16[16,256,1024,1]{2,1,3,0:T(8,128)(2,1)} fusion(bf16[16,256,1024]{2,1,0:T(8,128)(2,1)} %bitcast.61, bf16[15,256,1024]{2,1,0:T(8,128)(2,1)} %collective-permute-done, f32[1024]{0:T(1024)S(1)} %bitcast.77, f32[1024]{0:T(1024)S(1)} %bitcast.78, f32[1024]{0:T(1024)S(1)} %bitcast.64, f32[1024]{0:T(1024)S(1)} %bitcast.65, ...), kind=kLoop, calls=%fused_computation.51.clone.clone.clone.2 | loop fusion | flops 264241152 | bytes 24707072 | tf_op jit(solution)/shard_map/pcn,fin->cfpi/dot_general | solution.py:66
  239.7 8.2 %fusion.20 = bf16[16,256,2,256]{1,3,2,0:T(8,128)(2,1)S(1)} fusion(bf16[1,256,1024]{2,1,0:T(8,128)(2,1)S(1)} %get-tuple-element.42, bf16[1,256,1024]{2,1,0:T(8,128)(2,1)S(1)} %get-tuple-element.41, bf16[16,256,1024,1]{2,1,3,0:T(8,128)(2,1)} %fusion.41), kind=kOutput, calls=%fused_computation.56 | convolution fusion | flops 4299161600 | bytes 13631488 | tf_op jit(solution)/shard_map/pcn,fin->cfpi/dot_general | solution.py:66
  261.5 13.4 %collective-permute-done.2 = bf16[1,16,16,2,256]{4,1,0,3,2:T(8,128)(2,1)S(1)} collective-permute-done((bf16[1,16,16,2,256]{4,1,0,3,2:T(8,128)(2,1)S(1)}, bf16[1,16,16,2,256]{4,1,0,3,2:T(8,128)(2,1)S(1)}, u32[]{:S(2)}, u32[]{:S(2)}) %collective-permute-start.2) | collective-permute-done | bytes 262176 | tf_op jit(solution)/shard_map/ppermute | solution.py:21
  280.9 11.2 %broadcast_in_dim.32 = bf16[1,16,16,2,4096]{2,1,4,3,0:T(8,128)(2,1)} broadcast(bf16[]{:T(256)} %constant.17.clone.1), dimensions={} | broadcast | bytes 4194306 | tf_op jit(solution)/shard_map/broadcast_in_dim | solution.py:17
  293.7 4.5 copy.9
  307.8 4.5 copy.12
  313.9 4.5 copy.13
  321.8 4.5 copy.14
  326.7 4.5 copy.15
  331.2 4.5 copy.16
  342.2 22.9 %collective-permute-done.9 = bf16[1,16,16,2,256]{4,1,0,3,2:T(8,128)(2,1)} collective-permute-done((bf16[1,16,16,2,256]{4,1,0,3,2:T(8,128)(2,1)}, bf16[1,16,16,2,256]{4,1,0,3,2:T(8,128)(2,1)}, u32[]{:S(2)}, u32[]{:S(2)}) %collective-permute-start.9) | collective-permute-done | bytes 262176 | tf_op jit(solution)/shard_map/ppermute | solution.py:21
  365.8 4.5 copy.17
  375.4 5.6 collective-permute-done.10
  381.0 4.5 copy.18
  394.6 4.7 copy.19
  404.4 4.5 copy.20
  415.5 4.5 copy.21
  438.8 36.7 %gather_fusion = bf16[1024,16,16,2,4]{2,1,4,3,0:T(8,128)(2,1)} fusion(bf16[16,16,2,4,1024]{1,0,4,3,2:T(8,128)(2,1)} %bitcast.60, s32[1024]{0:T(1024)S(1)} %fusion.31), kind=kCustom, calls=%fused_computation | custom fusion | bytes 8392704 | tf_op jit(solution)/shard_map/jit(_take)/gather | solution.py:74
  475.5 35.7 %copy.24 = bf16[16,16,2,4,1024]{4,0,3,2,1:T(8,128)(2,1)} copy(bf16[16,16,2,4,1024]{1,0,3,2,4:T(8,128)(2,1)} %bitcast.59) | data formatting | bytes 8388608 | tf_op jit(solution)/shard_map/jit(_take)/gather | solution.py:74
  511.2 22.7 %broadcast_select_fusion = bf16[16,16,2,4,1024]{1,0,3,2,4:T(8,128)(2,1)} fusion(pred[1024]{0:T(1024)(128)(4,1)S(1)} %compare_and_fusion, bf16[1024,16,16,2,4]{2,1,4,3,0:T(8,128)(2,1)} %gather_fusion), kind=kLoop, calls=%fused_computation.33 | loop fusion | flops 2097152 | bytes 8389632 | tf_op jit(solution)/shard_map/jit(_take)/select_n | solution.py:74
  534.0 4.5 bitcast_select_fusion
  538.5 25.2 %fusion.33 = (bf16[16,16,1,4,1024]{1,0,3,2,4:T(8,128)(2,1)}, bf16[16,16,1,4,1024]{1,0,3,2,4:T(8,128)(2,1)}) fusion(bf16[16,16,2,4,1024]{1,0,3,2,4:T(8,128)(2,1)} %broadcast_select_fusion), kind=kLoop, calls=%fused_computation.107 | loop fusion | bytes 8388608 | tf_op jit(solution)/shard_map/slice | solution.py:77
  563.7 21.9 %copy.28 = bf16[16,16,1,4,1024]{4,3,1,0,2:T(4,128)(2,1)} copy(bf16[16,16,1,4,1024]{1,0,3,2,4:T(8,128)(2,1)} %get-tuple-element.7) | data formatting | bytes 4194304 | tf_op jit(solution)/shard_map/slice | solution.py:77
  588.4 21.9 %copy.27 = bf16[16,16,1,4,1024]{4,3,1,0,2:T(4,128)(2,1)} copy(bf16[16,16,1,4,1024]{1,0,3,2,4:T(8,128)(2,1)} %get-tuple-element.8) | data formatting | bytes 4194304 | tf_op jit(solution)/shard_map/slice | solution.py:76
  614.2 24.8 %fusion.35 = f32[16,1024,1024]{2,1,0:T(8,128)} fusion(bf16[16,64,1024]{2,1,0:T(8,128)(2,1)} %reshape_squeeze.6, bf16[16,64,1024]{2,1,0:T(8,128)(2,1)S(1)} %reshape_squeeze.7), kind=kOutput, calls=%fused_computation.109 | convolution fusion | flops 2147483648 | bytes 71303168 | tf_op jit(solution)/shard_map/kra,krb->kab/dot_general | solution.py:79
  639.0 62.9 %copy.29 = f32[16,1024,1024]{1,2,0:T(8,128)} copy(f32[16,1024,1024]{2,1,0:T(8,128)} %fusion.35) | data formatting | bytes 134217728 | tf_op jit(solution)/shard_map/kra,krb->kab/dot_general | solution.py:79
  701.9 64.2 %fusion.2 = bf16[16,1024,1024]{2,1,0:T(8,128)(2,1)} fusion(f32[16,1024,1024]{2,1,0:T(8,128)} %fusion.35, f32[16,1024,1024]{1,2,0:T(8,128)} %copy.29, pred[1024,1024]{1,0:T(8,128)(4,1)S(1)} %copy-done, bf16[16,128,1024]{2,0,1:T(8,128)(2,1)} %bitcast_select_fusion), kind=kOutput, calls=%fused_computation.4 | convolution fusion | flops 4362076160 | bytes 173015040 | tf_op jit(solution)/shard_map/kra,krb->kab/dot_general | solution.py:78
  (72 shorter events, 96.4 us)
Async XLA Ops:
  7.7 173.7 %collective-permute-start = (bf16[15,256,1024]{2,1,0:T(8,128)(2,1)}, bf16[15,256,1024]{2,1,0:T(8,128)(2,1)}, u32[]{:S(2)}, u32[]{:S(2)}) collective-permute-start(bf16[15,256,1024]{2,1,0:T(8,128)(2,1)} %slice_bitcast_fusion), channel_id=1, source_target_pairs={{0,4},{1,5},{2,6},{3,7},{4,8},{5,9},{6,10},{7,11},{8,12},{9,13},{1... | collective-permute-start | bytes 23592968 | tf_op jit(solution)/shard_map/ppermute | solution.py:29
  249.5 8.5 %collective-permute-start.3 = (bf16[1,16,16,2,256]{4,1,0,3,2:T(8,128)(2,1)S(1)}, bf16[1,16,16,2,256]{4,1,0,3,2:T(8,128)(2,1)S(1)}, u32[]{:S(2)}, u32[]{:S(2)}) collective-permute-start(bf16[1,16,16,2,256]{4,1,0,3,2:T(8,128)(2,1)S(1)} %get-tuple-element.21), channel_id=1, source_target_pairs={{0,3},{1,2},{2,1},{3,0},{4,7},{5,6},{6,5},{7,4},{8,11},{9,10},{10,... | collective-permute-start | bytes 786440 | tf_op jit(solution)/shard_map/ppermute | solution.py:21
  249.6 25.4 %collective-permute-start.2 = (bf16[1,16,16,2,256]{4,1,0,3,2:T(8,128)(2,1)S(1)}, bf16[1,16,16,2,256]{4,1,0,3,2:T(8,128)(2,1)S(1)}, u32[]{:S(2)}, u32[]{:S(2)}) collective-permute-start(bf16[1,16,16,2,256]{4,1,0,3,2:T(8,128)(2,1)S(1)} %get-tuple-element.22), channel_id=1, source_target_pairs={{0,2},{1,3},{2,0},{3,1},{4,6},{5,7},{6,4},{7,5},{8,10},{9,11},{10,... | collective-permute-start | bytes 786440 | tf_op jit(solution)/shard_map/ppermute | solution.py:21
  251.0 26.1 %collective-permute-start.1 = (bf16[1,16,16,2,256]{4,1,0,3,2:T(8,128)(2,1)S(1)}, bf16[1,16,16,2,256]{4,1,0,3,2:T(8,128)(2,1)S(1)}, u32[]{:S(2)}, u32[]{:S(2)}) collective-permute-start(bf16[1,16,16,2,256]{4,1,0,3,2:T(8,128)(2,1)S(1)} %get-tuple-element.23), channel_id=1, source_target_pairs={{0,1},{1,0},{2,3},{3,2},{4,5},{5,4},{6,7},{7,6},{8,9},{9,8},{10,11... | collective-permute-start | bytes 786440 | tf_op jit(solution)/shard_map/ppermute | solution.py:21
  251.3 79.8 %collective-permute-start.8 = (bf16[1,16,16,2,256]{4,1,0,3,2:T(8,128)(2,1)}, bf16[1,16,16,2,256]{4,1,0,3,2:T(8,128)(2,1)}, u32[]{:S(2)}, u32[]{:S(2)}) collective-permute-start(bf16[1,16,16,2,256]{4,1,0,3,2:T(8,128)(2,1)} %get-tuple-element.16), channel_id=1, source_target_pairs={{0,8},{1,9},{2,10},{3,11},{4,12},{5,13},{6,14},{7,15},{8,0},{9,1},... | collective-permute-start | bytes 786440 | tf_op jit(solution)/shard_map/ppermute | solution.py:21
  254.9 71.4 %collective-permute-start.7 = (bf16[1,16,16,2,256]{4,1,0,3,2:T(8,128)(2,1)}, bf16[1,16,16,2,256]{4,1,0,3,2:T(8,128)(2,1)}, u32[]{:S(2)}, u32[]{:S(2)}) collective-permute-start(bf16[1,16,16,2,256]{4,1,0,3,2:T(8,128)(2,1)} %get-tuple-element.17), channel_id=1, source_target_pairs={{0,7},{1,6},{2,5},{3,4},{4,3},{5,2},{6,1},{7,0},{8,15},{9,14},{10,... | collective-permute-start | bytes 786440 | tf_op jit(solution)/shard_map/ppermute | solution.py:21
  258.0 20.8 %copy-start.4 = (bf16[1,16,16,2,256]{4,1,0,3,2:T(8,128)(2,1)}, bf16[1,16,16,2,256]{4,1,0,3,2:T(8,128)(2,1)S(1)}, u32[]{:S(2)}) copy-start(bf16[1,16,16,2,256]{4,1,0,3,2:T(8,128)(2,1)S(1)} %collective-permute-done.3) | copy-start | bytes 786436
  258.0 60.4 %collective-permute-start.6 = (bf16[1,16,16,2,256]{4,1,0,3,2:T(8,128)(2,1)}, bf16[1,16,16,2,256]{4,1,0,3,2:T(8,128)(2,1)}, u32[]{:S(2)}, u32[]{:S(2)}) collective-permute-start(bf16[1,16,16,2,256]{4,1,0,3,2:T(8,128)(2,1)} %get-tuple-element.18), channel_id=1, source_target_pairs={{0,6},{1,7},{2,4},{3,5},{4,2},{5,3},{6,0},{7,1},{8,14},{9,15},{10,... | collective-permute-start | bytes 786440 | tf_op jit(solution)/shard_map/ppermute | solution.py:21
  274.9 3.9 copy-start.5
  274.9 37.3 %collective-permute-start.5 = (bf16[1,16,16,2,256]{4,1,0,3,2:T(8,128)(2,1)}, bf16[1,16,16,2,256]{4,1,0,3,2:T(8,128)(2,1)}, u32[]{:S(2)}, u32[]{:S(2)}) collective-permute-start(bf16[1,16,16,2,256]{4,1,0,3,2:T(8,128)(2,1)} %get-tuple-element.19), channel_id=1, source_target_pairs={{0,5},{1,4},{2,7},{3,6},{4,1},{5,0},{6,3},{7,2},{8,13},{9,12},{10,... | collective-permute-start | bytes 786440 | tf_op jit(solution)/shard_map/ppermute | solution.py:21
  277.1 1.7 copy-start.7
  277.1 27.9 %collective-permute-start.4 = (bf16[1,16,16,2,256]{4,1,0,3,2:T(8,128)(2,1)}, bf16[1,16,16,2,256]{4,1,0,3,2:T(8,128)(2,1)}, u32[]{:S(2)}, u32[]{:S(2)}) collective-permute-start(bf16[1,16,16,2,256]{4,1,0,3,2:T(8,128)(2,1)} %get-tuple-element.20), channel_id=1, source_target_pairs={{0,4},{1,5},{2,6},{3,7},{4,0},{5,1},{6,2},{7,3},{8,12},{9,13},{10,... | collective-permute-start | bytes 786440 | tf_op jit(solution)/shard_map/ppermute | solution.py:21
  280.8 17.3 %copy-start.6 = (bf16[1,16,16,2,256]{4,1,0,3,2:T(8,128)(2,1)S(1)}, bf16[1,16,16,2,256]{4,1,0,3,2:T(8,128)(2,1)}, u32[]{:S(2)}) copy-start(bf16[1,16,16,2,256]{4,1,0,3,2:T(8,128)(2,1)} %copy-done.5) | copy-start | bytes 786436
  301.3 79.7 %copy-start.3 = (bf16[1,16,16,2,256]{4,1,0,3,2:T(8,128)(2,1)S(1)}, bf16[1,16,16,2,256]{4,1,0,3,2:T(8,128)(2,1)}, u32[]{:S(2)}) copy-start(bf16[1,16,16,2,256]{4,1,0,3,2:T(8,128)(2,1)} %get-tuple-element.13) | copy-start | bytes 786436
  305.0 128.5 %collective-permute-start.15 = (bf16[1,16,16,2,256]{4,1,0,3,2:T(8,128)(2,1)S(1)}, bf16[1,16,16,2,256]{4,1,0,3,2:T(8,128)(2,1)}, u32[]{:S(2)}, u32[]{:S(2)}) collective-permute-start(bf16[1,16,16,2,256]{4,1,0,3,2:T(8,128)(2,1)S(1)} %get-tuple-element.9), channel_id=1, source_target_pairs={{0,15},{1,14},{2,13},{3,12},{4,11},{5,10},{6,9},{7,8},{8,7},{9,6},... | collective-permute-start | bytes 786440 | tf_op jit(solution)/shard_map/ppermute | solution.py:21
  312.2 112.6 %collective-permute-start.14 = (bf16[1,16,16,2,256]{4,1,0,3,2:T(8,128)(2,1)S(1)}, bf16[1,16,16,2,256]{4,1,0,3,2:T(8,128)(2,1)}, u32[]{:S(2)}, u32[]{:S(2)}) collective-permute-start(bf16[1,16,16,2,256]{4,1,0,3,2:T(8,128)(2,1)S(1)} %get-tuple-element.10), channel_id=1, source_target_pairs={{0,14},{1,15},{2,12},{3,13},{4,10},{5,11},{6,8},{7,9},{8,6},{9,7},... | collective-permute-start | bytes 786440 | tf_op jit(solution)/shard_map/ppermute | solution.py:21
  318.4 97.1 %collective-permute-start.13 = (bf16[1,16,16,2,256]{4,1,0,3,2:T(8,128)(2,1)S(1)}, bf16[1,16,16,2,256]{4,1,0,3,2:T(8,128)(2,1)}, u32[]{:S(2)}, u32[]{:S(2)}) collective-permute-start(bf16[1,16,16,2,256]{4,1,0,3,2:T(8,128)(2,1)S(1)} %get-tuple-element.11), channel_id=1, source_target_pairs={{0,13},{1,12},{2,15},{3,14},{4,9},{5,8},{6,11},{7,10},{8,5},{9,4},... | collective-permute-start | bytes 786440 | tf_op jit(solution)/shard_map/ppermute | solution.py:21
  326.3 78.1 %collective-permute-start.12 = (bf16[1,16,16,2,256]{4,1,0,3,2:T(8,128)(2,1)S(1)}, bf16[1,16,16,2,256]{4,1,0,3,2:T(8,128)(2,1)}, u32[]{:S(2)}, u32[]{:S(2)}) collective-permute-start(bf16[1,16,16,2,256]{4,1,0,3,2:T(8,128)(2,1)S(1)} %get-tuple-element.12), channel_id=1, source_target_pairs={{0,12},{1,13},{2,14},{3,15},{4,8},{5,9},{6,10},{7,11},{8,4},{9,5},... | collective-permute-start | bytes 786440 | tf_op jit(solution)/shard_map/ppermute | solution.py:21
  331.1 33.9 %collective-permute-start.9 = (bf16[1,16,16,2,256]{4,1,0,3,2:T(8,128)(2,1)}, bf16[1,16,16,2,256]{4,1,0,3,2:T(8,128)(2,1)}, u32[]{:S(2)}, u32[]{:S(2)}) collective-permute-start(bf16[1,16,16,2,256]{4,1,0,3,2:T(8,128)(2,1)} %get-tuple-element.15), channel_id=1, source_target_pairs={{0,9},{1,8},{2,11},{3,10},{4,13},{5,12},{6,15},{7,14},{8,1},{9,0},... | collective-permute-start | bytes 786440 | tf_op jit(solution)/shard_map/ppermute | solution.py:21
  365.0 15.9 %collective-permute-start.10 = (bf16[1,16,16,2,256]{4,1,0,3,2:T(8,128)(2,1)}, bf16[1,16,16,2,256]{4,1,0,3,2:T(8,128)(2,1)}, u32[]{:S(2)}, u32[]{:S(2)}) collective-permute-start(bf16[1,16,16,2,256]{4,1,0,3,2:T(8,128)(2,1)} %get-tuple-element.14), channel_id=1, source_target_pairs={{0,10},{1,11},{2,8},{3,9},{4,14},{5,15},{6,12},{7,13},{8,2},{9,3},... | collective-permute-start | bytes 786440 | tf_op jit(solution)/shard_map/ppermute | solution.py:21
  372.0 27.3 %copy-start.1 = (bf16[1,16,16,2,256]{2,1,4,3,0:T(8,128)(2,1)S(1)}, bf16[1,16,16,2,256]{2,1,4,3,0:T(8,128)(2,1)}, u32[]{:S(2)}) copy-start(bf16[1,16,16,2,256]{2,1,4,3,0:T(8,128)(2,1)} %copy.15) | copy-start | bytes 786436
  381.0 13.6 %collective-permute-start.11 = (bf16[1,16,16,2,256]{4,1,0,3,2:T(8,128)(2,1)S(1)}, bf16[1,16,16,2,256]{4,1,0,3,2:T(8,128)(2,1)}, u32[]{:S(2)}, u32[]{:S(2)}) collective-permute-start(bf16[1,16,16,2,256]{4,1,0,3,2:T(8,128)(2,1)S(1)} %copy-done.3), channel_id=1, source_target_pairs={{0,11},{1,10},{2,9},{3,8},{4,15},{5,14},{6,13},{7,12},{8,3},{9,2},... | collective-permute-start | bytes 786440 | tf_op jit(solution)/shard_map/ppermute | solution.py:21
  401.0 19.0 %copy-start.2 = (bf16[1,16,16,2,256]{2,1,4,3,0:T(8,128)(2,1)S(1)}, bf16[1,16,16,2,256]{2,1,4,3,0:T(8,128)(2,1)}, u32[]{:S(2)}) copy-start(bf16[1,16,16,2,256]{2,1,4,3,0:T(8,128)(2,1)} %copy.19) | copy-start | bytes 786436
  639.0 62.9 %copy-start = (pred[1024,1024]{1,0:T(8,128)(4,1)S(1)}, pred[1024,1024]{1,0:T(8,128)(4,1)}, u32[]{:S(2)}) copy-start(pred[1024,1024]{1,0:T(8,128)(4,1)} %iota_compare_fusion) | copy-start | bytes 3145732
